TPU v7x, 32 devices: a whole 2x2x4 slice. The times are simulated.
32 devices in a mesh: space: 8 (over y, x, core), dp: 4 (over z).
Axes of the slice: x: 2, y: 2, z: 4, core: 2. Of those that a mesh axis runs over, the one named last changes fastest.
Arguments:
- block_in: bfloat16 [4, 8, 56, 56, 128], P('dp', 'space'), may hold values from -6 to 6
- weights: bfloat16 [3, 3, 128, 128], replicated, may hold values from -0.1875 to 0.1875
- out_bias: float32 [128], replicated, may hold values from -3 to 3
- adjacency: int32 [8, 8, 2], P('space'), may hold values from 0 to 7, as said below
- cotangent: bfloat16 [4, 8, 56, 56, 128], P('dp', 'space'), may hold values from -6 to 6
Outputs:
- block_out: bfloat16 [4, 8, 56, 56, 128], P('dp', 'space')
- weight_grad: float32 [3, 3, 128, 128], replicated
- grad_in: bfloat16 [4, 8, 56, 56, 128], P('dp', 'space')
Inputs may be any that keep to these rules, and one draw needn't show every extreme that they name: adjacency[t, e] = (p, f) for e < 4 means that adjacency[p, f] = (t, e): edges are glued in pairs; entries 4 + k hold a tile and corner k' with adjacency[p, 4 + k'] = (t, k), corners glued in pairs. The corner pairing need not follow the edge pairing. Every edge and every corner of every tile appears exactly once as a partner. Column 1 lies in 0..3.
All inputs are finite; a program needn't handle non-finite values.
Results may differ from a plain program's by a relative error of at most 0.0031.
Values may be sent and summed in bfloat16 or wider, within the bound.
A program may use at most 64 MiB of HBM per device.

v0:
```python
import jax
import jax.numpy as jnp
from jax import lax
from jax.sharding import PartitionSpec as P


def tile_edges(field):
    top_rim = field[0, :, :]
    right_rim = field[:, -1, :]
    bottom_rim = jnp.flip(field[-1, :, :], 0)
    left_rim = jnp.flip(field[:, 0, :], 0)
    return jnp.stack([top_rim, right_rim, bottom_rim, left_rim], 0)


def tile_corners(field):
    return jnp.stack([field[0, 0, :], field[0, -1, :], field[-1, -1, :], field[-1, 0, :]], 0)


def assemble(field, near_edges, near_corners):
    top_row = jnp.concatenate([near_corners[0:1], jnp.flip(near_edges[0], 0), near_corners[1:2]], 0)
    bottom_row = jnp.concatenate([near_corners[3:4], near_edges[2], near_corners[2:3]], 0)
    middle = jnp.concatenate(
        [near_edges[3][:, None], field, jnp.flip(near_edges[1], 0)[:, None]], 1
    )
    return jnp.concatenate([top_row[None], middle, bottom_row[None]], 0)


def conv_forward(padded, weights):
    side = padded.shape[0] - 2
    width = padded.shape[2]
    running = jnp.zeros((side * side, weights.shape[3]), jnp.float32)
    for row_off in range(3):
        for col_off in range(3):
            window = padded[row_off : row_off + side, col_off : col_off + side].reshape(
                side * side, width
            )
            running = running + jnp.dot(
                window, weights[row_off, col_off], preferred_element_type=jnp.float32
            )
    return running.reshape(side, side, -1)


def conv_backward(padded, grad_out, weights):
    side = padded.shape[0] - 2
    width = padded.shape[2]
    grad_rows = grad_out.reshape(side * side, -1)
    grad_pad = jnp.zeros(padded.shape, jnp.float32)
    kernel_rows = []
    for row_off in range(3):
        kernel_cols = []
        for col_off in range(3):
            window = padded[row_off : row_off + side, col_off : col_off + side].reshape(
                side * side, width
            )
            kernel_cols.append(jnp.dot(window.T, grad_rows, preferred_element_type=jnp.float32))
            back = jnp.dot(
                grad_rows, weights[row_off, col_off].T, preferred_element_type=jnp.float32
            )
            grad_pad = grad_pad + jnp.pad(
                back.reshape(side, side, width),
                ((row_off, 2 - row_off), (col_off, 2 - col_off), (0, 0)),
            )
        kernel_rows.append(jnp.stack(kernel_cols, 0))
    return (jnp.stack(kernel_rows, 0), grad_pad)


def rim_grads(grad_pad):
    top_rim = grad_pad[0, 1:-1]
    right_rim = grad_pad[1:-1, -1]
    bottom_rim = jnp.flip(grad_pad[-1, 1:-1], 0)
    left_rim = jnp.flip(grad_pad[1:-1, 0], 0)
    rim_edges = jnp.stack([top_rim, right_rim, bottom_rim, left_rim], 0).astype(jnp.bfloat16)
    rim_corners = jnp.stack(
        [grad_pad[0, 0], grad_pad[0, -1], grad_pad[-1, -1], grad_pad[-1, 0]], 0
    ).astype(jnp.bfloat16)
    return (rim_edges, rim_corners)


def add_back(interior, back_edges, back_corners):
    edge_vals = back_edges.astype(jnp.float32)
    corner_vals = back_corners.astype(jnp.float32)
    interior = interior.at[0, :].add(jnp.flip(edge_vals[0], 0))
    interior = interior.at[:, -1].add(jnp.flip(edge_vals[1], 0))
    interior = interior.at[-1, :].add(edge_vals[2])
    interior = interior.at[:, 0].add(edge_vals[3])
    interior = interior.at[0, 0].add(corner_vals[0])
    interior = interior.at[0, -1].add(corner_vals[1])
    interior = interior.at[-1, -1].add(corner_vals[2])
    interior = interior.at[-1, 0].add(corner_vals[3])
    return interior


def glue(edge_cells, corner_cells, link_rows, backward):
    edge_tile = link_rows[0:4, 0]
    edge_side = link_rows[0:4, 1]
    corner_tile = link_rows[4:8, 0]
    corner_side = link_rows[4:8, 1]
    tile_count = lax.axis_size("space")
    tile_ids = jnp.arange(tile_count, dtype=jnp.int32)
    edge_hit = edge_tile[None, :] == tile_ids[:, None]
    corner_hit = corner_tile[None, :] == tile_ids[:, None]
    outgoing = jnp.where(
        edge_hit[:, :, None, None], edge_cells[None], jnp.zeros((), edge_cells.dtype)
    )
    outgoing_corners = jnp.where(
        corner_hit[:, :, None], corner_cells[None], jnp.zeros((), corner_cells.dtype)
    )
    if backward:
        arrived, arrived_corners = (
            lax.all_to_all(outgoing, "space", split_axis=0, concat_axis=0, tiled=True),
            lax.all_to_all(outgoing_corners, "space", split_axis=0, concat_axis=0, tiled=True),
        )
    else:
        arrived, arrived_corners = (
            lax.all_to_all(outgoing, "space", split_axis=0, concat_axis=0, tiled=True),
            lax.all_to_all(outgoing_corners, "space", split_axis=0, concat_axis=0, tiled=True),
        )
    return (arrived[edge_tile, edge_side], arrived_corners[corner_tile, corner_side])


def per_device(block_in, weights, out_bias, adjacency, cotangent):
    inputs = block_in[0, 0]
    link_rows = adjacency[0]
    activation = jax.nn.silu(inputs.astype(jnp.float32)).astype(jnp.bfloat16)
    near_edges, near_corners = glue(
        tile_edges(activation), tile_corners(activation), link_rows, False
    )
    padded = assemble(activation, near_edges, near_corners)
    conv_sum = conv_forward(padded, weights)
    result = (inputs.astype(jnp.float32) + conv_sum + out_bias).astype(jnp.bfloat16)
    grad_out = cotangent[0, 0]
    local_kernel, grad_pad = conv_backward(padded, grad_out, weights)
    rim_edges, rim_corners = rim_grads(grad_pad)
    back_edges, back_corners = glue(rim_edges, rim_corners, link_rows, True)
    act_grad = add_back(grad_pad[1:-1, 1:-1], back_edges, back_corners)
    input_f = inputs.astype(jnp.float32)
    sigmoid_x = jax.nn.sigmoid(input_f)
    grad_in = (
        grad_out.astype(jnp.float32) + act_grad * sigmoid_x * (1.0 + input_f * (1.0 - sigmoid_x))
    ).astype(jnp.bfloat16)
    weight_grad = lax.psum(local_kernel, ("space", "dp"))
    return (result[None, None], weight_grad, grad_in[None, None])


def solution(mesh):
    placed = (
        P("dp", "space", None, None, None),
        P(),
        P(),
        P("space", None, None),
        P("dp", "space", None, None, None),
    )
    return jax.shard_map(
        per_device,
        mesh=mesh,
        in_specs=placed,
        out_specs=(P("dp", "space", None, None, None), P(), P("dp", "space", None, None, None)),
        check_vma=False,
    )
```

profile of v0, /device:TPU:0, one launch (start us, length us, event | category | flops | bytes accessed | tf_op | source)
XLA Modules:
  0.0 241.1 jit_solution(15127318088615724658)
XLA Ops:
  7.2 1.8 fusion.20
  13.6 1.2 pad_add_fusion
  14.8 1.0 copy.103
  15.8 0.7 fusion.79
  16.8 0.7 broadcast_select_fusion.2
  17.5 5.2 %all-to-all-start.3 = ((bf16[8,4,128]{2,1,0:T(4,128)(2,1)}), bf16[8,4,128]{2,1,0:T(4,128)(2,1)}, u32[]{:S(2)}, u32[]{:S(2)}) async-start(bf16[8,4,128]{2,1,0:T(4,128)(2,1)} %broadcast_select_fusion.2), calls=%async_computation.3 | async-start | bytes 16384 | tf_op jit(solution)/shard_map/all_to_all | solution.py:111
  22.6 0.9 slice.471
  23.6 0.7 slice_bitcast_fusion.4
  24.3 0.6 slice_bitcast_fusion.3
  24.9 0.6 copy.66
  25.5 0.6 rev.31
  26.2 0.7 rev.30
  26.9 0.7 iota_compare_fusion
  27.6 0.7 pad_maximum_fusion.5
  28.3 0.9 broadcast_select_fusion
  29.2 4.2 %all-to-all-start.2 = ((bf16[8,4,56,128]{3,2,1,0:T(8,128)(2,1)}), bf16[8,4,56,128]{3,2,1,0:T(8,128)(2,1)}, u32[]{:S(2)}, u32[]{:S(2)}) async-start(bf16[8,4,56,128]{3,2,1,0:T(8,128)(2,1)} %broadcast_select_fusion), calls=%async_computation.2 | async-start | bytes 917504 | tf_op jit(solution)/shard_map/all_to_all | solution.py:110
  34.1 1.5 copy.102
  35.6 1.0 copy.45
  36.6 0.7 fusion.93
  37.2 0.8 and_reduce_fusion
  38.0 1.3 gather_fusion.3
  39.3 3.2 %all-to-all-done.2 = bf16[8,4,56,128]{3,2,1,0:T(8,128)(2,1)} async-done(((bf16[8,4,56,128]{3,2,1,0:T(8,128)(2,1)}), bf16[8,4,56,128]{3,2,1,0:T(8,128)(2,1)}, u32[]{:S(2)}, u32[]{:S(2)}) %all-to-all-start.2) | async-done | bytes 458784 | tf_op jit(solution)/shard_map/all_to_all | solution.py:110
  42.5 2.2 gather_fusion.2
  44.7 0.8 convert_element_type.76
  45.6 1.4 slice.479
  46.9 0.6 slice_bitcast_fusion.1
  47.6 1.4 rev.32
  48.9 1.4 slice_add_fusion.2
  50.3 1.7 scatter-add.26
  52.0 1.4 fusion.67
  53.4 1.0 slice_add_fusion
  54.4 1.8 scatter-add.30
  56.1 0.8 fusion.66
  57.5 1.3 scatter-add.34
  58.8 2.6 %broadcast_select_fusion.4 = f32[1,1,128]{2,0,1:T(1,128)S(1)} fusion(pred[]{:T(512)} %and_reduce_fusion, f32[56,56,128]{2,0,1:T(8,128)} %scatter-add.34, s32[]{:T(128)} %bitcast.94, s32[]{:T(128)} %bitcast.95, f32[4,128]{1,0:T(4,128)S(1)} %convert_element_type.77), kind=kLoop, calls=%fused_computation.136 | loop fusion | flops 256 | bytes 1545 | tf_op jit(solution)/shard_map/select.13
  61.3 2.5 %scatter-add.35 = f32[56,56,128]{2,0,1:T(8,128)} dynamic-update-slice(f32[56,56,128]{2,0,1:T(8,128)} %scatter-add.34, f32[1,1,128]{2,0,1:T(1,128)S(1)} %broadcast_select_fusion.4, s32[]{:T(128)} %bitcast.94, s32[]{:T(128)} %bitcast.95, s32[]{:T(128)} %constant.227.clone.1) | dynamic-update-slice | bytes 1028 | tf_op jit(solution)/shard_map/scatter-add | solution.py:87
  63.9 0.7 slice_add_fusion.4
  64.6 1.3 scatter-add.36
  65.8 0.7 slice_add_fusion.3
  66.5 1.3 scatter-add.39
  67.8 2.2 fusion.19
  70.2 0.7 broadcast_select_fusion.3
  70.9 3.3 %all-to-all-start = ((bf16[8,4,128]{2,1,0:T(4,128)(2,1)}), bf16[8,4,128]{2,1,0:T(4,128)(2,1)S(1)}, u32[]{:S(2)}, u32[]{:S(2)}) async-start(bf16[8,4,128]{2,1,0:T(4,128)(2,1)} %broadcast_select_fusion.3), calls=%async_computation | async-start | bytes 16384 | tf_op jit(solution)/shard_map/all_to_all | solution.py:116
  74.3 0.9 broadcast_select_fusion.1
  75.1 3.7 %all-to-all-done = bf16[8,4,128]{2,1,0:T(4,128)(2,1)S(1)} async-done(((bf16[8,4,128]{2,1,0:T(4,128)(2,1)}), bf16[8,4,128]{2,1,0:T(4,128)(2,1)S(1)}, u32[]{:S(2)}, u32[]{:S(2)}) %all-to-all-start) | async-done | bytes 8224 | tf_op jit(solution)/shard_map/all_to_all | solution.py:116
  78.9 4.1 %all-to-all-start.1 = ((bf16[8,4,56,128]{3,2,1,0:T(8,128)(2,1)}), bf16[8,4,56,128]{3,2,1,0:T(8,128)(2,1)}, u32[]{:S(2)}, u32[]{:S(2)}) async-start(bf16[8,4,56,128]{3,2,1,0:T(8,128)(2,1)} %broadcast_select_fusion.1), calls=%async_computation.1 | async-start | bytes 917504 | tf_op jit(solution)/shard_map/all_to_all | solution.py:115
  83.2 2.2 convolution_bitcast_fusion.4
  85.4 1.0 copy.74
  87.0 5.1 %all-to-all-done.1 = bf16[8,4,56,128]{3,2,1,0:T(8,128)(2,1)} async-done(((bf16[8,4,56,128]{3,2,1,0:T(8,128)(2,1)}), bf16[8,4,56,128]{3,2,1,0:T(8,128)(2,1)}, u32[]{:S(2)}, u32[]{:S(2)}) %all-to-all-start.1) | async-done | bytes 458784 | tf_op jit(solution)/shard_map/all_to_all | solution.py:115
  92.1 1.6 gather_fusion.1
  93.9 0.7 pad_maximum_fusion
  95.2 0.7 copy-done.15
  95.9 1.5 fusion.46
  99.9 0.9 copy-done.6
  104.6 0.9 pad_maximum_fusion.3
  105.8 1.8 convolution_add_fusion.7
  108.0 0.8 copy-done.7
  109.1 0.8 copy-done.13
  110.6 0.8 copy-done.11
  111.8 0.8 copy-done.9
  112.9 0.8 copy-done.3
  114.7 1.0 copy.73
  115.7 116.7 %all-reduce.11.cloned.1.call-done = f32[3,3,128,128]{3,2,1,0:T(8,128)} async-done(((f32[3,3,128,128]{3,2,1,0:T(8,128)}), f32[3,3,128,128]{3,2,1,0:T(8,128)}) %all-reduce.11.cloned.1.call-update) | async-done | bytes 589840 | tf_op jit(solution)/shard_map/psum | solution.py:141
  232.4 1.9 copy.114
  (116 shorter events, 17.5 us)
Async XLA Ops:
  7.2 1.8 copy-start.14
  7.2 1.8 copy-start
  14.8 1.1 copy-start.24
  15.8 1.0 copy-start.16
  15.8 17.6 %copy-start.1 = (bf16[1,1,56,56,128]{4,3,2,1,0:T(8,128)(2,1)S(1)}, bf16[1,1,56,56,128]{4,3,2,1,0:T(8,128)(2,1)}, u32[]{:S(2)}) copy-start(bf16[1,1,56,56,128]{4,3,2,1,0:T(8,128)(2,1)} %param.21) | copy-start | bytes 2408452
  16.8 6.8 %copy-start.22 = (pred[8,4]{1,0:T(8,128)(4,1)}, pred[8,4]{1,0:T(8,128)(4,1)S(1)}, u32[]{:S(2)}) copy-start(pred[8,4]{1,0:T(8,128)(4,1)S(1)} %iota_compare_fusion.1) | copy-start | bytes 100
  17.5 11.7 %all-to-all-start.3 = ((bf16[8,4,128]{2,1,0:T(4,128)(2,1)}), bf16[8,4,128]{2,1,0:T(4,128)(2,1)}, u32[]{:S(2)}, u32[]{:S(2)}) async-start(bf16[8,4,128]{2,1,0:T(4,128)(2,1)} %broadcast_select_fusion.2), calls=%async_computation.3 | async-start | bytes 16384 | tf_op jit(solution)/shard_map/all_to_all | solution.py:111
  27.6 6.5 %copy-start.20 = (pred[8,4]{1,0:T(8,128)(4,1)}, pred[8,4]{1,0:T(8,128)(4,1)S(1)}, u32[]{:S(2)}) copy-start(pred[8,4]{1,0:T(8,128)(4,1)S(1)} %iota_compare_fusion) | copy-start | bytes 100
  29.2 13.3 %all-to-all-start.2 = ((bf16[8,4,56,128]{3,2,1,0:T(8,128)(2,1)}), bf16[8,4,56,128]{3,2,1,0:T(8,128)(2,1)}, u32[]{:S(2)}, u32[]{:S(2)}) async-start(bf16[8,4,56,128]{3,2,1,0:T(8,128)(2,1)} %broadcast_select_fusion), calls=%async_computation.2 | async-start | bytes 917504 | tf_op jit(solution)/shard_map/all_to_all | solution.py:110
  33.8 1.7 copy-start.12
  35.6 1.7 copy-start.25
  35.6 2.4 %copy-start.19 = (s32[4]{0:T(128)S(1)}, s32[4]{0:T(128)}, u32[]{:S(2)}) copy-start(s32[4]{0:T(128)} %get-tuple-element.139) | copy-start | bytes 52
  45.6 1.4 copy-start.17
  67.8 2.4 copy-start.23
  67.8 6.5 %copy-start.21 = (pred[8,4]{1,0:T(8,128)(4,1)S(1)}, pred[8,4]{1,0:T(8,128)(4,1)}, u32[]{:S(2)}) copy-start(pred[8,4]{1,0:T(8,128)(4,1)} %copy-done.20) | copy-start | bytes 100
  70.9 8.0 %all-to-all-start = ((bf16[8,4,128]{2,1,0:T(4,128)(2,1)}), bf16[8,4,128]{2,1,0:T(4,128)(2,1)S(1)}, u32[]{:S(2)}, u32[]{:S(2)}) async-start(bf16[8,4,128]{2,1,0:T(4,128)(2,1)} %broadcast_select_fusion.3), calls=%async_computation | async-start | bytes 16384 | tf_op jit(solution)/shard_map/all_to_all | solution.py:116
  78.9 13.2 %all-to-all-start.1 = ((bf16[8,4,56,128]{3,2,1,0:T(8,128)(2,1)}), bf16[8,4,56,128]{3,2,1,0:T(8,128)(2,1)}, u32[]{:S(2)}, u32[]{:S(2)}) async-start(bf16[8,4,56,128]{3,2,1,0:T(8,128)(2,1)} %broadcast_select_fusion.1), calls=%async_computation.1 | async-start | bytes 917504 | tf_op jit(solution)/shard_map/all_to_all | solution.py:115
  83.0 149.4 %all-reduce.11.cloned.1.call-start = ((), (), s32[]{:S(2)}) async-start(), calls=%async_computation.4 | async-start | bytes 1179648 | tf_op jit(solution)/shard_map/psum | solution.py:141
  94.9 1.0 copy-start.15
  98.4 0.9 copy-start.4
  99.9 0.9 copy-start.6
  101.8 0.9 copy-start.2
  102.7 0.9 copy-start.8
  103.1 1.4 copy-start.18
  103.6 0.9 copy-start.10
  104.5 1.4 copy-start.5
  107.6 1.1 copy-start.7
  108.8 1.1 copy-start.13
  110.2 1.2 copy-start.11
  111.4 1.1 copy-start.9
  112.5 1.1 copy-start.3
  113.7 0.7 copy-start.26
Sparse Core Ops, SparseCore 0:
  105.6 126.7 all-reduce.10
where the time goes:
time: 243 us; the launch traced here: 241 us
  waiting for transfers between devices  129 us (53%)
  local copies, waits for them, and re-layouts  42 us (17%)
  other arithmetic  21.2 us (9%)
  matrix products  17.5 us (7%)
  starting transfers between devices  17 us (7%)
  between operations  14.7 us (6%)
    psum x1, waiting for transfers between devices, per_device(): weight_grad = lax.psum(local_kernel, ('space', 'dp'))  117 us
    unnamed x60, local copies, waits for them, and re-layouts  13.6 us
    all_to_all x2, starting transfers between devices, glue(): lax.all_to_all(outgoing_corners, 'space', split_axis=0, concat_axis=0, ti...  8.5 us
    all_to_all x2, starting transfers between devices, glue(): lax.all_to_all(outgoing, 'space', split_axis=0, concat_axis=0, tiled=True)  8.32 us
    all_to_all x2, waiting for transfers between devices, glue(): lax.all_to_all(outgoing, 'space', split_axis=0, concat_axis=0, tiled=True)  8.3 us
    dot_general x9, matrix products, conv_backward(): jnp.dot(grad_rows, weights[row_off, col_off].T, preferred_element_type=jn...  6.31 us
    dot_general x9, matrix products, conv_forward(): jnp.dot(window, weights[row_off, col_off], preferred_element_type=jnp.flo...  5.74 us
    dot_general x9, matrix products, conv_backward(): jnp.dot(window.T, grad_rows, preferred_element_type=jnp.float32)  5.49 us
  transfers between devices with their start and end apart: 5, of which 4 were waited for; matrix products, arithmetic and copies ran while one was open for 9% of the time, Pallas kernels for 0%

commit v1 on v0

--- a/solution.py
+++ b/solution.py
@@ -138,7 +138,8 @@
     grad_in = (
         grad_out.astype(jnp.float32) + act_grad * sigmoid_x * (1.0 + input_f * (1.0 - sigmoid_x))
     ).astype(jnp.bfloat16)
-    weight_grad = lax.psum(local_kernel, ("space", "dp"))
+    partial = lax.psum(local_kernel, "dp")
+    weight_grad = lax.psum(partial, "space")
     return (result[None, None], weight_grad, grad_in[None, None])
 
 

time: 243 us -> 213 us (0.88)
  waiting for transfers between devices: 129 us -> 98.8 us
    psum x1 -> x2, waiting for transfers between devices: 117 us -> 86.7 us  [the longest x1 56.4 us: per_device(): weight_grad = lax.psum(partial, 'space')]
  transfers between devices with their start and end apart: 5 -> 6, of which waited for: 4 -> 5; matrix products, arithmetic and copies ran while one was open for 9% -> 11% of each run, Pallas kernels for 0% -> 0%
where the time goes in v1:
time: 213 us; the launch traced here: 211 us
  waiting for transfers between devices  98.8 us (46%)
  local copies, waits for them, and re-layouts  41.6 us (20%)
  other arithmetic  21.2 us (10%)
  matrix products  17.5 us (8%)
  starting transfers between devices  17.1 us (8%)
  between operations  14.7 us (7%)
    psum x1, waiting for transfers between devices, per_device(): weight_grad = lax.psum(partial, 'space')  56.4 us
    psum x1, waiting for transfers between devices, per_device(): partial = lax.psum(local_kernel, 'dp')  30.4 us
    unnamed x60, local copies, waits for them, and re-layouts  13.2 us
    all_to_all x2, starting transfers between devices, glue(): lax.all_to_all(outgoing_corners, 'space', split_axis=0, concat_axis=0, ti...  8.5 us
    all_to_all x2, starting transfers between devices, glue(): lax.all_to_all(outgoing, 'space', split_axis=0, concat_axis=0, tiled=True)  8.32 us
    all_to_all x2, waiting for transfers between devices, glue(): lax.all_to_all(outgoing, 'space', split_axis=0, concat_axis=0, tiled=True)  8.3 us
    dot_general x9, matrix products, conv_backward(): jnp.dot(grad_rows, weights[row_off, col_off].T, preferred_element_type=jn...  6.31 us
    dot_general x9, matrix products, conv_forward(): jnp.dot(window, weights[row_off, col_off], preferred_element_type=jnp.flo...  5.74 us
  transfers between devices with their start and end apart: 6, of which 5 were waited for; matrix products, arithmetic and copies ran while one was open for 11% of the time, Pallas kernels for 0%

profile of v1, /device:TPU:0, one launch (start us, length us, event | category | flops | bytes accessed | tf_op | source)
XLA Modules:
  0.0 210.9 jit_solution(16226935869807019806)
XLA Ops:
  7.2 1.8 fusion.20
  13.6 1.2 pad_add_fusion
  14.8 1.0 copy.103
  15.8 0.7 fusion.79
  16.8 0.7 broadcast_select_fusion.2
  17.5 5.2 %all-to-all-start.3 = ((bf16[8,4,128]{2,1,0:T(4,128)(2,1)}), bf16[8,4,128]{2,1,0:T(4,128)(2,1)}, u32[]{:S(2)}, u32[]{:S(2)}) async-start(bf16[8,4,128]{2,1,0:T(4,128)(2,1)} %broadcast_select_fusion.2), calls=%async_computation.3 | async-start | bytes 16384 | tf_op jit(solution)/shard_map/all_to_all | solution.py:111
  22.6 0.9 slice.471
  23.6 0.7 slice_bitcast_fusion.4
  24.3 0.6 slice_bitcast_fusion.3
  25.5 0.6 rev.31
  26.2 0.7 rev.30
  26.9 0.7 iota_compare_fusion
  27.6 0.7 pad_maximum_fusion.5
  28.3 0.9 broadcast_select_fusion
  29.2 4.2 %all-to-all-start.2 = ((bf16[8,4,56,128]{3,2,1,0:T(8,128)(2,1)}), bf16[8,4,56,128]{3,2,1,0:T(8,128)(2,1)}, u32[]{:S(2)}, u32[]{:S(2)}) async-start(bf16[8,4,56,128]{3,2,1,0:T(8,128)(2,1)} %broadcast_select_fusion), calls=%async_computation.2 | async-start | bytes 917504 | tf_op jit(solution)/shard_map/all_to_all | solution.py:110
  34.1 1.5 copy.102
  35.6 1.0 copy.45
  36.6 0.7 fusion.93
  37.2 0.8 and_reduce_fusion
  38.0 1.3 gather_fusion.3
  39.3 3.2 %all-to-all-done.2 = bf16[8,4,56,128]{3,2,1,0:T(8,128)(2,1)} async-done(((bf16[8,4,56,128]{3,2,1,0:T(8,128)(2,1)}), bf16[8,4,56,128]{3,2,1,0:T(8,128)(2,1)}, u32[]{:S(2)}, u32[]{:S(2)}) %all-to-all-start.2) | async-done | bytes 458784 | tf_op jit(solution)/shard_map/all_to_all | solution.py:110
  42.5 2.2 %gather_fusion.2 = bf16[4,56,128]{2,1,0:T(8,128)(2,1)} fusion(bf16[8,4,56,128]{3,2,1,0:T(8,128)(2,1)} %all-to-all-done.2, s32[4]{0:T(128)S(1)} %get-tuple-element.140), kind=kCustom, calls=%fused_computation.2 | custom fusion | bytes 114720 | tf_op jit(solution)/shard_map/gather | solution.py:118
  44.7 0.8 convert_element_type.76
  45.6 1.4 slice.479
  46.9 0.6 slice_bitcast_fusion.1
  47.6 1.4 rev.32
  48.9 1.4 slice_add_fusion.2
  50.3 1.7 scatter-add.26
  52.0 1.4 fusion.67
  53.4 1.0 slice_add_fusion
  54.4 1.8 scatter-add.30
  56.1 0.8 fusion.66
  57.5 1.3 scatter-add.34
  58.8 2.6 %broadcast_select_fusion.4 = f32[1,1,128]{2,0,1:T(1,128)S(1)} fusion(pred[]{:T(512)} %and_reduce_fusion, f32[56,56,128]{2,0,1:T(8,128)} %scatter-add.34, s32[]{:T(128)} %bitcast.94, s32[]{:T(128)} %bitcast.95, f32[4,128]{1,0:T(4,128)S(1)} %convert_element_type.77), kind=kLoop, calls=%fused_computation.136 | loop fusion | flops 256 | bytes 1545 | tf_op jit(solution)/shard_map/select.13
  61.3 2.5 %scatter-add.35 = f32[56,56,128]{2,0,1:T(8,128)} dynamic-update-slice(f32[56,56,128]{2,0,1:T(8,128)} %scatter-add.34, f32[1,1,128]{2,0,1:T(1,128)S(1)} %broadcast_select_fusion.4, s32[]{:T(128)} %bitcast.94, s32[]{:T(128)} %bitcast.95, s32[]{:T(128)} %constant.227.clone.1) | dynamic-update-slice | bytes 1028 | tf_op jit(solution)/shard_map/scatter-add | solution.py:87
  63.9 0.7 slice_add_fusion.4
  64.6 1.3 scatter-add.36
  65.8 0.7 slice_add_fusion.3
  66.5 1.3 scatter-add.39
  67.8 2.2 %fusion.19 = (bf16[1,1,56,56,128]{4,2,3,1,0:T(8,128)(2,1)S(1)}, bf16[56,56,128]{2,0,1:T(8,128)(2,1)S(1)}) fusion(f32[56,56,128]{2,0,1:T(8,128)} %scatter-add.39, bf16[1,1,56,56,128]{4,3,2,1,0:T(8,128)(2,1)S(1)} %copy-done, bf16[1,1,56,56,128]{4,3,2,1,0:T(8,128)(2,1)S(1)} %copy-done.1), kind=kLoop, calls=%fused_computation.49 | loop fusion | flops 5619712 | bytes 4816896 | tf_op jit(solution)/shard_map/broadcast_in_dim | solution.py:143
  70.2 0.7 broadcast_select_fusion.3
  70.9 3.3 %all-to-all-start = ((bf16[8,4,128]{2,1,0:T(4,128)(2,1)}), bf16[8,4,128]{2,1,0:T(4,128)(2,1)S(1)}, u32[]{:S(2)}, u32[]{:S(2)}) async-start(bf16[8,4,128]{2,1,0:T(4,128)(2,1)} %broadcast_select_fusion.3), calls=%async_computation | async-start | bytes 16384 | tf_op jit(solution)/shard_map/all_to_all | solution.py:116
  74.3 0.9 broadcast_select_fusion.1
  75.1 3.7 %all-to-all-done = bf16[8,4,128]{2,1,0:T(4,128)(2,1)S(1)} async-done(((bf16[8,4,128]{2,1,0:T(4,128)(2,1)}), bf16[8,4,128]{2,1,0:T(4,128)(2,1)S(1)}, u32[]{:S(2)}, u32[]{:S(2)}) %all-to-all-start) | async-done | bytes 8224 | tf_op jit(solution)/shard_map/all_to_all | solution.py:116
  78.9 4.1 %all-to-all-start.1 = ((bf16[8,4,56,128]{3,2,1,0:T(8,128)(2,1)}), bf16[8,4,56,128]{3,2,1,0:T(8,128)(2,1)}, u32[]{:S(2)}, u32[]{:S(2)}) async-start(bf16[8,4,56,128]{3,2,1,0:T(8,128)(2,1)} %broadcast_select_fusion.1), calls=%async_computation.1 | async-start | bytes 917504 | tf_op jit(solution)/shard_map/all_to_all | solution.py:115
  83.2 2.2 %convolution_bitcast_fusion.4 = f32[1,128,128]{2,1,0:T(8,128)} fusion(bf16[56,56,128]{2,1,0:T(8,128)(2,1)S(1)} %bitcast.281, bf16[1,1,56,56,128]{4,2,3,1,0:T(8,128)(2,1)} %copy-done.12), kind=kOutput, calls=%fused_computation.38 | convolution fusion | flops 102760448 | bytes 1671168 | tf_op jit(solution)/shard_map/dot_general | solution.py:55
  85.4 1.0 copy.74
  87.0 5.1 %all-to-all-done.1 = bf16[8,4,56,128]{3,2,1,0:T(8,128)(2,1)} async-done(((bf16[8,4,56,128]{3,2,1,0:T(8,128)(2,1)}), bf16[8,4,56,128]{3,2,1,0:T(8,128)(2,1)}, u32[]{:S(2)}, u32[]{:S(2)}) %all-to-all-start.1) | async-done | bytes 458784 | tf_op jit(solution)/shard_map/all_to_all | solution.py:115
  92.1 1.6 gather_fusion.1
  93.9 0.7 pad_maximum_fusion
  95.2 0.7 copy-done.15
  95.9 1.5 fusion.46
  99.9 0.9 copy-done.6
  104.6 0.9 pad_maximum_fusion.3
  105.8 1.8 convolution_add_fusion.7
  108.0 0.8 copy-done.7
  109.1 0.8 copy-done.13
  110.6 0.8 copy-done.11
  111.8 0.8 copy-done.9
  112.9 0.8 copy-done.3
  114.0 30.4 %all-reduce.12.cloned.1.call-done = f32[3,3,128,128]{3,2,1,0:T(8,128)} async-done(((f32[3,3,128,128]{3,2,1,0:T(8,128)}), f32[3,3,128,128]{3,2,1,0:T(8,128)}) %all-reduce.12.cloned.1.call-update) | async-done | bytes 589840 | tf_op jit(solution)/shard_map/psum | solution.py:141
  144.8 1.0 copy.73
  145.8 56.4 %all-reduce.14.cloned.1.call-done = f32[3,3,128,128]{3,2,1,0:T(8,128)} async-done(((f32[3,3,128,128]{3,2,1,0:T(8,128)}), f32[3,3,128,128]{3,2,1,0:T(8,128)}) %all-reduce.14.cloned.1.call-update) | async-done | bytes 589840 | tf_op jit(solution)/shard_map/psum | solution.py:142
  202.2 1.9 copy.115
  (119 shorter events, 17.8 us)
Async XLA Ops:
  7.2 1.8 copy-start.14
  7.2 1.8 copy-start
  14.8 1.1 copy-start.24
  15.8 1.0 copy-start.16
  15.8 17.6 %copy-start.1 = (bf16[1,1,56,56,128]{4,3,2,1,0:T(8,128)(2,1)S(1)}, bf16[1,1,56,56,128]{4,3,2,1,0:T(8,128)(2,1)}, u32[]{:S(2)}) copy-start(bf16[1,1,56,56,128]{4,3,2,1,0:T(8,128)(2,1)} %param.21) | copy-start | bytes 2408452
  16.8 6.8 %copy-start.22 = (pred[8,4]{1,0:T(8,128)(4,1)}, pred[8,4]{1,0:T(8,128)(4,1)S(1)}, u32[]{:S(2)}) copy-start(pred[8,4]{1,0:T(8,128)(4,1)S(1)} %iota_compare_fusion.1) | copy-start | bytes 100
  17.5 11.7 %all-to-all-start.3 = ((bf16[8,4,128]{2,1,0:T(4,128)(2,1)}), bf16[8,4,128]{2,1,0:T(4,128)(2,1)}, u32[]{:S(2)}, u32[]{:S(2)}) async-start(bf16[8,4,128]{2,1,0:T(4,128)(2,1)} %broadcast_select_fusion.2), calls=%async_computation.3 | async-start | bytes 16384 | tf_op jit(solution)/shard_map/all_to_all | solution.py:111
  27.6 6.5 %copy-start.20 = (pred[8,4]{1,0:T(8,128)(4,1)}, pred[8,4]{1,0:T(8,128)(4,1)S(1)}, u32[]{:S(2)}) copy-start(pred[8,4]{1,0:T(8,128)(4,1)S(1)} %iota_compare_fusion) | copy-start | bytes 100
  29.2 13.3 %all-to-all-start.2 = ((bf16[8,4,56,128]{3,2,1,0:T(8,128)(2,1)}), bf16[8,4,56,128]{3,2,1,0:T(8,128)(2,1)}, u32[]{:S(2)}, u32[]{:S(2)}) async-start(bf16[8,4,56,128]{3,2,1,0:T(8,128)(2,1)} %broadcast_select_fusion), calls=%async_computation.2 | async-start | bytes 917504 | tf_op jit(solution)/shard_map/all_to_all | solution.py:110
  33.8 1.7 copy-start.12
  35.6 1.7 copy-start.25
  35.6 2.4 %copy-start.19 = (s32[4]{0:T(128)S(1)}, s32[4]{0:T(128)}, u32[]{:S(2)}) copy-start(s32[4]{0:T(128)} %get-tuple-element.139) | copy-start | bytes 52
  45.6 1.4 copy-start.17
  67.8 2.4 %copy-start.23 = (pred[8,4]{1,0:T(8,128)(4,1)S(1)}, pred[8,4]{1,0:T(8,128)(4,1)}, u32[]{:S(2)}) copy-start(pred[8,4]{1,0:T(8,128)(4,1)} %copy-done.22) | copy-start | bytes 100
  67.8 6.5 %copy-start.21 = (pred[8,4]{1,0:T(8,128)(4,1)S(1)}, pred[8,4]{1,0:T(8,128)(4,1)}, u32[]{:S(2)}) copy-start(pred[8,4]{1,0:T(8,128)(4,1)} %copy-done.20) | copy-start | bytes 100
  70.9 8.0 %all-to-all-start = ((bf16[8,4,128]{2,1,0:T(4,128)(2,1)}), bf16[8,4,128]{2,1,0:T(4,128)(2,1)S(1)}, u32[]{:S(2)}, u32[]{:S(2)}) async-start(bf16[8,4,128]{2,1,0:T(4,128)(2,1)} %broadcast_select_fusion.3), calls=%async_computation | async-start | bytes 16384 | tf_op jit(solution)/shard_map/all_to_all | solution.py:116
  78.9 13.2 %all-to-all-start.1 = ((bf16[8,4,56,128]{3,2,1,0:T(8,128)(2,1)}), bf16[8,4,56,128]{3,2,1,0:T(8,128)(2,1)}, u32[]{:S(2)}, u32[]{:S(2)}) async-start(bf16[8,4,56,128]{3,2,1,0:T(8,128)(2,1)} %broadcast_select_fusion.1), calls=%async_computation.1 | async-start | bytes 917504 | tf_op jit(solution)/shard_map/all_to_all | solution.py:115
  83.0 61.4 %all-reduce.12.cloned.1.call-start = ((), (), s32[]{:S(2)}) async-start(), calls=%async_computation.4 | async-start | bytes 1179648 | tf_op jit(solution)/shard_map/psum | solution.py:141
  94.9 1.0 copy-start.15
  98.4 0.9 copy-start.4
  99.9 0.9 copy-start.6
  101.8 0.9 copy-start.2
  102.7 0.9 copy-start.8
  103.1 1.4 copy-start.18
  103.6 0.9 copy-start.10
  104.5 1.4 copy-start.5
  105.5 96.7 %all-reduce.14.cloned.1.call-start = ((), (), s32[]{:S(2)}) async-start(), calls=%async_computation.5 | async-start | bytes 1179648 | tf_op jit(solution)/shard_map/psum | solution.py:142
  107.6 1.1 copy-start.7
  108.8 1.1 copy-start.13
  110.2 1.1 copy-start.11
  111.4 1.1 copy-start.9
  112.5 1.1 copy-start.3
  113.7 30.8 %copy-start.26 = (f32[128]{0:T(128)S(1)}, f32[128]{0:T(128)}, u32[]{:S(2)}) copy-start(f32[128]{0:T(128)} %param.23) | copy-start | bytes 1540
Sparse Core Ops, SparseCore 0:
  105.6 38.7 all-reduce.11
  147.5 54.5 all-reduce.13
